TPU v7x, 32 devices: a whole 2x2x4 slice. The times are simulated.
32 devices in a mesh: pts: 4 (over x, core), atom: 8 (over z, y).
Axes of the slice: x: 2, y: 2, z: 4, core: 2. Of those that a mesh axis runs over, the one named last changes fastest.
Arguments:
- points: bfloat16 [131072, 256], P(('pts', 'atom')), may hold values from -6 to 6
- atoms: bfloat16 [4096, 256], P('atom'), may hold values from -6 to 6
- kept: int32 [1024, 4], P(('pts', 'atom')), may hold values from 0 to 11, as said below
- point_logw: float32 [131072], P(('pts', 'atom')), may hold values from -4 to 4
- atom_logw: float32 [4096], P('atom'), may hold values from -4 to 4
- epsilons: float32 [2], replicated, may hold values from 0.004 to 0.008
- relaxation: float32 [1], replicated, may hold values from 0.02 to 0.2
Outputs:
- point_potential: float32 [131072], P(('pts', 'atom'))
- atom_potential: float32 [4096], P('atom')
- point_log_mass: float32 [131072], P(('pts', 'atom'))
Inputs may be any that keep to these rules, and one draw needn't show every extreme that they name: `kept`: the entries of one row are distinct.
All inputs are finite; a program needn't handle non-finite values.
Results may differ from a plain program's by a relative error of at most 0.0003.
Values may be sent and summed in bfloat16 or wider, within the bound.
A program may use at most 64 MiB of HBM per device.

v0:
```python
import functools
import math

import jax
import jax.numpy as jnp
from jax import lax
from jax.experimental import pallas as pl
from jax.experimental.pallas import tpu as pltpu
from jax.sharding import PartitionSpec as P

MESH = pl.DeviceIdType.MESH
lowest = -1e30
LOG2E = 1.0 / math.log(2.0)
LN2 = math.log(2.0)
GROUP = 4
STRIP = 32


def kernel(
    npts,
    natom,
    kept_h,
    eps_h,
    relax_h,
    points_h,
    atoms_h,
    plogw_h,
    alogw_h,
    pot_out,
    apot_out,
    mass_out,
    kept_s,
    eps_s,
    relax_s,
    plogw,
    pts_v,
    win,
    wlogw,
    x_s,
    spn,
    l2,
    a2,
    krow,
    mrow,
    srow,
    b2,
    san,
    acc,
    part,
    rb,
    lsem,
    hsend,
    hrecv,
    fsend,
    frecv,
    gsend,
    grecv,
    esend,
    erecv,
):
    blocks, rows, depth = pts_v.shape
    keep = krow.shape[0] // blocks
    panel = alogw_h.shape[0]
    iters = eps_s.shape[0]
    half = panel // 2
    mine, here = lax.axis_index("pts"), lax.axis_index("atom")
    up, down = lax.rem(here + 1, natom), lax.rem(here + natom - 1, natom)
    core = lax.rem(mine, 2)
    partner = mine + 1 - 2 * core

    local = []
    for n, (src, dst) in enumerate(
        (
            (kept_h, kept_s),
            (plogw_h, plogw),
            (eps_h, eps_s),
            (relax_h, relax_s),
            (alogw_h, wlogw.at[1]),
            (points_h, pts_v),
            (atoms_h, win.at[pl.ds(panel, panel)]),
        )
    ):
        local.append(pltpu.make_async_copy(src, dst, lsem.at[n]))
    for copy in local:
        copy.start()

    partners = []
    for o in (-2, -1, 0, 1, 2):
        for t in range(npts):
            if o == 0 and t == 0:
                continue
            partners.append((o, t))

    def target(o, t):
        return (lax.rem(mine + t, npts), lax.rem(here - o + natom, natom))

    barrier = pltpu.get_barrier_semaphore()
    for o, t in partners:
        pl.semaphore_signal(barrier, inc=1, device_id=target(o, t), device_id_type=MESH)
    pl.semaphore_wait(barrier, len(partners))

    halo, small = [], []
    mine_half = pl.ds(core * half, half)
    for side, (slot, to) in enumerate(((0, up), (2, down))):
        halo.append(
            pltpu.make_async_remote_copy(
                src_ref=atoms_h.at[mine_half],
                dst_ref=win.at[pl.ds(slot * panel + core * half, half)],
                send_sem=hsend.at[side],
                recv_sem=hrecv.at[side],
                device_id=(mine, to),
                device_id_type=MESH,
            )
        )
        small.append(
            pltpu.make_async_remote_copy(
                src_ref=alogw_h,
                dst_ref=wlogw.at[slot],
                send_sem=gsend.at[side],
                recv_sem=grecv.at[side],
                device_id=(mine, to),
                device_id_type=MESH,
            )
        )
    for copy in halo + small:
        copy.start()

    for copy in local:
        copy.wait()

    def prepare(q, carry):
        p = pts_v[q].astype(jnp.float32)
        sq = jnp.sum(p * p, axis=1, keepdims=True) * (0.5 / depth)
        spn[q] = jnp.broadcast_to(sq, (rows, 128))
        lw = jnp.broadcast_to(plogw[pl.ds(q, 1), :], (rows, 128)) * LOG2E
        l2[q] = jnp.transpose(lw)
        for k in range(keep):
            krow[pl.ds(q * keep + k, 1), :] = jnp.full((1, 128), kept_s[k, q], jnp.int32)
        return carry

    lax.fori_loop(0, blocks, prepare, 0)

    def norms(slot):
        for w in range(slot * panel, (slot + 1) * panel):
            a = win[w].astype(jnp.float32)
            sq = jnp.sum(a * a, axis=1, keepdims=True) * (0.5 / depth)
            san[pl.ds(w, 1), :] = jnp.transpose(jnp.broadcast_to(sq, (rows, 128)))[0:1, :]

    norms(1)
    forward = []
    for side, slot in enumerate((0, 2)):
        halo[side].wait_recv()
        piece = pl.ds(slot * panel + core * half, half)
        forward.append(
            pltpu.make_async_remote_copy(
                src_ref=win.at[piece],
                dst_ref=win.at[piece],
                send_sem=fsend.at[side],
                recv_sem=frecv.at[side],
                device_id=(partner, here),
                device_id_type=MESH,
            )
        )
        forward[side].start()
    for side, slot in enumerate((0, 2)):
        forward[side].wait()
        norms(slot)
    for copy in halo:
        copy.wait_send()
    for copy in small:
        copy.wait()

    strength = relax_s[0]
    lanes = lax.broadcasted_iota(jnp.int32, (rows, 128), 1)
    acc[...] = jnp.zeros_like(acc)

    def bias(inv_eps, j, pot):
        block = pl.ds(j * panel, panel)
        b2[block, :] = LOG2E * (wlogw[j] + (pot - san[block, :]) * inv_eps)

    def point_lse(q, ratio, brow, strip):
        t = x_s[q, strip, :]
        if ratio is not None:
            t = t * ratio
            x_s[q, strip, :] = t
        t = t + brow
        top = jnp.max(t, axis=1, keepdims=True)
        total = jnp.sum(jnp.exp2(t - top), axis=1, keepdims=True)
        return jnp.broadcast_to(top + jnp.log2(total), (STRIP, 128))

    def bias_row(q):
        return jnp.concatenate(
            [b2[pl.ds(kept_s[k, q], 1), :] for k in range(keep)], axis=1
        )

    for it in range(iters):
        eps = eps_s[it]
        inv_eps = jnp.ones((1, 128), jnp.float32) / jnp.full((1, 128), eps, jnp.float32)
        factor = strength / (strength + eps)
        scale = (LOG2E / depth) * inv_eps[0:1, 0:1]
        if it == 0:
            for j in range(3):
                bias(inv_eps, j, jnp.zeros((panel, 128), jnp.float32))
        ratio = None if it == 0 else eps_s[it - 1] * inv_eps[0:1, 0:1]
        last = it == iters - 1

        def one(q):
            if it == 0:
                chosen = jnp.concatenate(
                    [win[kept_s[k, q]] for k in range(keep)], axis=0
                )
                x_s[q] = scale * lax.dot_general(
                    pts_v[q],
                    chosen,
                    (((1,), (1,)), ((), ())),
                    preferred_element_type=jnp.float32,
                )
            brow = bias_row(q)
            for r in range(rows // STRIP):
                strip = pl.ds(r * STRIP, STRIP)
                lse = point_lse(q, ratio, brow, strip)
                sp = spn[q, strip, :]
                pot = factor * (sp - (eps * LN2) * lse)
                a2[q, strip, :] = l2[q, strip, :] + (pot - sp) * (LOG2E * inv_eps)
                if last:
                    acc[strip, :] = jnp.where(lanes[:STRIP] == q, pot, acc[strip, :])
            for k in range(keep):
                u = x_s[q, :, pl.ds(k * 128, 128)] + a2[q]
                top = jnp.max(u, axis=0, keepdims=True)
                total = jnp.sum(jnp.exp2(u - top), axis=0, keepdims=True)
                mrow[pl.ds(q * keep + k, 1), :] = top
                srow[pl.ds(q * keep + k, 1), :] = total

        def step(g, carry):
            for i in range(GROUP):
                one(g * GROUP + i)
            return carry

        lax.fori_loop(0, blocks // GROUP, step, 0)

        member, m = krow[...], mrow[...]
        tops, shift = [], jnp.zeros_like(m)
        for w in range(3 * panel):
            chosen = member == w
            tops.append(jnp.max(jnp.where(chosen, m, lowest), axis=0, keepdims=True))
            shift = jnp.where(chosen, tops[w], shift)
        terms = srow[...] * jnp.exp2(m - shift)
        for w in range(3 * panel):
            total = jnp.sum(jnp.where(member == w, terms, 0.0), axis=0, keepdims=True)
            part[it, w // panel, pl.ds(w % panel, 1), :] = jnp.where(
                total > 0.0, tops[w] + jnp.log2(total), lowest
            )
        rb[it, 2, mine] = part[it]

        copies = []
        for n, (o, t) in enumerate(partners):
            low, high = max(0, -o), min(3, 3 - o)
            copies.append(
                pltpu.make_async_remote_copy(
                    src_ref=part.at[it, pl.ds(low, high - low)],
                    dst_ref=rb.at[it, o + 2, mine, pl.ds(low + o, high - low)],
                    send_sem=esend.at[it, n],
                    recv_sem=erecv.at[it, n],
                    device_id=target(o, t),
                    device_id_type=MESH,
                )
            )
        for copy in copies:
            copy.start()
        if last:
            pot_out[...] = jnp.transpose(acc[...])[:blocks]
        for copy in copies:
            copy.wait()

        next_eps = eps_s[min(it + 1, iters - 1)]
        next_inv = jnp.ones((1, 128), jnp.float32) / jnp.full((1, 128), next_eps, jnp.float32)
        for j in range(3):
            terms = [
                rb[it, o + 2, s, j] for o in range(j - 2, j + 1) for s in range(npts)
            ]
            top = functools.reduce(jnp.maximum, terms)
            total = functools.reduce(jnp.add, [jnp.exp2(term - top) for term in terms])
            lse = jnp.where(top > 0.5 * lowest, top + jnp.log2(total), -jnp.inf)
            pot = factor * (san[pl.ds(j * panel, panel), :] - (eps * LN2) * lse)
            bias(next_inv, j, pot)
            if last and j == 1:
                apot_out[...] = pot

    def closing(g, carry):
        for i in range(GROUP):
            q = g * GROUP + i
            brow = bias_row(q)
            for r in range(rows // STRIP):
                strip = pl.ds(r * STRIP, STRIP)
                mass = (point_lse(q, None, brow, strip) + a2[q, strip, :]) * LN2
                acc[strip, :] = jnp.where(lanes[:STRIP] == q, mass, acc[strip, :])
        return carry

    lax.fori_loop(0, blocks // GROUP, closing, 0)
    mass_out[...] = jnp.transpose(acc[...])[:blocks]


def finish(pot, apot, mass, pot_out, apot_out, mass_out, sem):
    copies = [
        pltpu.make_async_copy(src, dst, sem.at[n])
        for n, (src, dst) in enumerate(
            ((pot, pot_out), (apot, apot_out), (mass, mass_out))
        )
    ]
    for copy in copies:
        copy.start()
    for copy in copies:
        copy.wait()


def per_device(points, atoms, kept, point_logw, atom_logw, epsilons, relaxation):
    depth = points.shape[1]
    blocks = points.shape[0] // 128
    panel = atoms.shape[0] // 128
    keep = kept.shape[1]
    iters = epsilons.shape[0]
    npts, natom = lax.axis_size("pts"), lax.axis_size("atom")
    partners = 5 * npts - 1
    f32, bf16 = jnp.float32, jnp.bfloat16
    vmem = pl.BlockSpec(memory_space=pltpu.VMEM)
    hbm = pl.BlockSpec(memory_space=pltpu.HBM)
    keep_here = functools.partial(
        pltpu.with_memory_space_constraint, memory_space=pltpu.HBM
    )
    pot, apot, mass = pl.pallas_call(
        functools.partial(kernel, npts, natom),
        out_shape=(
            jax.ShapeDtypeStruct((blocks, 128), f32),
            jax.ShapeDtypeStruct((panel, 128), f32),
            jax.ShapeDtypeStruct((blocks, 128), f32),
        ),
        in_specs=[hbm] * 7,
        out_specs=(vmem, vmem, vmem),
        scratch_shapes=[
            pltpu.SMEM((keep, blocks), jnp.int32),
            pltpu.SMEM((iters,), f32),
            pltpu.SMEM((1,), f32),
            pltpu.VMEM((blocks, 128), f32),
            pltpu.VMEM((blocks, 128, depth), bf16),
            pltpu.VMEM((3 * panel, 128, depth), bf16),
            pltpu.VMEM((3, panel, 128), f32),
            pltpu.VMEM((blocks, 128, keep * 128), f32),
            pltpu.VMEM((blocks, 128, 128), f32),
            pltpu.VMEM((blocks, 128, 128), f32),
            pltpu.VMEM((blocks, 128, 128), f32),
            pltpu.VMEM((blocks * keep, 128), jnp.int32),
            pltpu.VMEM((blocks * keep, 128), f32),
            pltpu.VMEM((blocks * keep, 128), f32),
            pltpu.VMEM((3 * panel, 128), f32),
            pltpu.VMEM((3 * panel, 128), f32),
            pltpu.VMEM((128, 128), f32),
            pltpu.VMEM((iters, 3, panel, 128), f32),
            pltpu.VMEM((iters, 5, npts, 3, panel, 128), f32),
            pltpu.SemaphoreType.DMA((7,)),
            pltpu.SemaphoreType.DMA((2,)),
            pltpu.SemaphoreType.DMA((2,)),
            pltpu.SemaphoreType.DMA((2,)),
            pltpu.SemaphoreType.DMA((2,)),
            pltpu.SemaphoreType.DMA((2,)),
            pltpu.SemaphoreType.DMA((2,)),
            pltpu.SemaphoreType.DMA((iters, partners)),
            pltpu.SemaphoreType.DMA((iters, partners)),
        ],
        compiler_params=pltpu.CompilerParams(
            collective_id=0, has_side_effects=True, vmem_limit_bytes=48 << 20
        ),
    )(
        keep_here(kept.T),
        keep_here(epsilons),
        relaxation,
        keep_here(points.reshape(blocks, 128, depth)),
        keep_here(atoms.reshape(panel, 128, depth)),
        keep_here(point_logw.reshape(blocks, 128)),
        keep_here(atom_logw.reshape(panel, 128)),
    )
    pot, apot, mass = pl.pallas_call(
        finish,
        out_shape=tuple(jax.ShapeDtypeStruct(v.shape, f32) for v in (pot, apot, mass)),
        in_specs=[vmem] * 3,
        out_specs=(hbm,) * 3,
        scratch_shapes=[pltpu.SemaphoreType.DMA((3,))],
        compiler_params=pltpu.CompilerParams(vmem_limit_bytes=48 << 20),
    )(pot, apot, mass)
    return pot.reshape(-1), apot.reshape(-1), mass.reshape(-1)


def solution(mesh):
    return jax.shard_map(
        per_device,
        mesh=mesh,
        in_specs=(
            P(("pts", "atom"), None),
            P("atom", None),
            P(("pts", "atom"), None),
            P(("pts", "atom")),
            P("atom"),
            P(),
            P(),
        ),
        out_specs=(P(("pts", "atom")), P("atom"), P(("pts", "atom"))),
        check_vma=False,
    )
```

profile of v0, /device:TPU:0, one launch (start us, length us, event | category | flops | bytes accessed | tf_op | source)
XLA Modules:
  0.0 43.0 jit_solution(2926786856673768287)
XLA Ops:
  1.3 41.1 %shard_map.94 = (f32[32,128]{1,0:T(8,128)S(1)}, f32[4,128]{1,0:T(4,128)S(1)}, f32[32,128]{1,0:T(8,128)S(1)}) custom-call(s32[4,32]{1,0:T(4,128)} %bitcast.11, f32[2]{0:T(128)} %eps_h.1, f32[1]{0:T(128)S(6)} %copy.10.relax_h, bf16[32,128,256]{2,1,0:T(8,128)(2,1)} %bitcast.8, bf16[4,128,256]{2,1,0:T(8,128)(2,1)} %bitcast.9, f32[32,128]{1,0:T(8,128)} %bitcast.10, ...), custom_call_target="tpu_custom_call" | custom-call | tf_op jit(solution)/shard_map/pallas_call | solution.py:330
  42.4 0.6 %shard_map.95 = (f32[32,128]{1,0:T(8,128)}, f32[4,128]{1,0:T(4,128)}, f32[32,128]{1,0:T(8,128)}) custom-call(f32[32,128]{1,0:T(8,128)S(1)} %get-tuple-element.9.pot, f32[4,128]{1,0:T(4,128)S(1)} %get-tuple-element.10.apot, f32[32,128]{1,0:T(8,128)S(1)} %get-tuple-element.11.mass), custom_call_target="tpu_custom_call" | custom-call | tf_op jit(solution)/shard_map/pallas_call | solution.py:381
where the time goes:
time: 43.2 us; the launch traced here: 43 us
  Pallas kernels  41.7 us (97%)
  between operations  1.29 us (3%)
    pallas_call x1, Pallas kernels, per_device(): pl.pallas_call(functools.partial(kernel, npts, natom), out_shape=(jax.Sha...  41.1 us

commit v1 on v0

--- a/solution.py
+++ b/solution.py
@@ -57,6 +57,8 @@
     grecv,
     esend,
     erecv,
+    near,
+    far,
 ):
     blocks, rows, depth = pts_v.shape
     keep = krow.shape[0] // blocks
@@ -94,10 +96,14 @@
     def target(o, t):
         return (lax.rem(mine + t, npts), lax.rem(here - o + natom, natom))
 
+    group = [target(0, t) for t in range(1, npts)]
+    sides = [(mine, up), (mine, down)]
     barrier = pltpu.get_barrier_semaphore()
-    for o, t in partners:
-        pl.semaphore_signal(barrier, inc=1, device_id=target(o, t), device_id_type=MESH)
-    pl.semaphore_wait(barrier, len(partners))
+    for device in sides + group:
+        pl.semaphore_signal(barrier, inc=1, device_id=device, device_id_type=MESH)
+    pl.semaphore_wait(barrier, len(sides) + len(group))
+    for device in group:
+        pl.semaphore_signal(near, inc=1, device_id=device, device_id_type=MESH)
 
     halo, small = [], []
     mine_half = pl.ds(core * half, half)
@@ -169,6 +175,10 @@
         copy.wait_send()
     for copy in small:
         copy.wait()
+
+    pl.semaphore_wait(near, len(group))
+    for device in sides:
+        pl.semaphore_signal(far, inc=1, device_id=device, device_id_type=MESH)
 
     strength = relax_s[0]
     lanes = lax.broadcasted_iota(jnp.int32, (rows, 128), 1)
@@ -265,6 +275,8 @@
                     device_id_type=MESH,
                 )
             )
+        if it == 0:
+            pl.semaphore_wait(far, len(sides))
         for copy in copies:
             copy.start()
         if last:
@@ -365,6 +377,8 @@
             pltpu.SemaphoreType.DMA((2,)),
             pltpu.SemaphoreType.DMA((iters, partners)),
             pltpu.SemaphoreType.DMA((iters, partners)),
+            pltpu.SemaphoreType.REGULAR,
+            pltpu.SemaphoreType.REGULAR,
         ],
         compiler_params=pltpu.CompilerParams(
             collective_id=0, has_side_effects=True, vmem_limit_bytes=48 << 20

time: 43.2 us -> 40.5 us (0.937)
  Pallas kernels: 41.7 us -> 39.1 us
    pallas_call x1, Pallas kernels: 41.1 us -> 38.4 us  [per_device(): pl.pallas_call(functools.partial(kernel, npts, natom), out_shape=(jax.Sha...]
where the time goes in v1:
time: 40.5 us; the launch traced here: 40.4 us
  Pallas kernels  39.1 us (97%)
  between operations  1.29 us (3%)
    pallas_call x1, Pallas kernels, per_device(): pl.pallas_call(functools.partial(kernel, npts, natom), out_shape=(jax.Sha...  38.4 us

profile of v1, /device:TPU:0, one launch (start us, length us, event | category | flops | bytes accessed | tf_op | source)
XLA Modules:
  0.0 40.4 jit_solution(5150836025358399086)
XLA Ops:
  1.3 38.4 %shard_map.94 = (f32[32,128]{1,0:T(8,128)S(1)}, f32[4,128]{1,0:T(4,128)S(1)}, f32[32,128]{1,0:T(8,128)S(1)}) custom-call(s32[4,32]{1,0:T(4,128)} %bitcast.11, f32[2]{0:T(128)} %eps_h.1, f32[1]{0:T(128)S(6)} %copy.10.relax_h, bf16[32,128,256]{2,1,0:T(8,128)(2,1)} %bitcast.8, bf16[4,128,256]{2,1,0:T(8,128)(2,1)} %bitcast.9, f32[32,128]{1,0:T(8,128)} %bitcast.10, ...), custom_call_target="tpu_custom_call" | custom-call | tf_op jit(solution)/shard_map/pallas_call | solution.py:342
  39.7 0.6 %shard_map.95 = (f32[32,128]{1,0:T(8,128)}, f32[4,128]{1,0:T(4,128)}, f32[32,128]{1,0:T(8,128)}) custom-call(f32[32,128]{1,0:T(8,128)S(1)} %get-tuple-element.9.pot, f32[4,128]{1,0:T(4,128)S(1)} %get-tuple-element.10.apot, f32[32,128]{1,0:T(8,128)S(1)} %get-tuple-element.11.mass), custom_call_target="tpu_custom_call" | custom-call | tf_op jit(solution)/shard_map/pallas_call | solution.py:395

commit v2 on v1

--- a/solution.py
+++ b/solution.py
@@ -12,8 +12,8 @@
 lowest = -1e30
 LOG2E = 1.0 / math.log(2.0)
 LN2 = math.log(2.0)
+STRIP = 32
 GROUP = 4
-STRIP = 32
 
 
 def kernel(
@@ -37,15 +37,16 @@
     win,
     wlogw,
     x_s,
-    spn,
-    l2,
+    base,
     a2,
+    spd,
     krow,
     mrow,
     srow,
     b2,
     san,
     acc,
+    acc2,
     part,
     rb,
     lsem,
@@ -60,8 +61,8 @@
     near,
     far,
 ):
-    blocks, rows, depth = pts_v.shape
-    keep = krow.shape[0] // blocks
+    blocks, rows, depth = points_h.shape
+    keep = kept_h.shape[0]
     panel = alogw_h.shape[0]
     iters = eps_s.shape[0]
     half = panel // 2
@@ -78,7 +79,7 @@
             (eps_h, eps_s),
             (relax_h, relax_s),
             (alogw_h, wlogw.at[1]),
-            (points_h, pts_v),
+            (points_h, pts_v.at[pl.ds(0, blocks)]),
             (atoms_h, win.at[pl.ds(panel, panel)]),
         )
     ):
@@ -134,17 +135,32 @@
     for copy in local:
         copy.wait()
 
+    lanes = lax.broadcasted_iota(jnp.int32, (rows, 128), 1)
+    strength = relax_s[0]
+    factors, weights = [], []
+    for it in range(iters):
+        eps = eps_s[it]
+        inv_eps = jnp.ones((1, 128), jnp.float32) / jnp.full((1, 128), eps, jnp.float32)
+        factors.append(strength / (strength + eps))
+        weights.append((factors[it] - 1.0) * LOG2E * inv_eps)
+    acc[...] = jnp.zeros_like(acc)
+    acc2[...] = jnp.zeros_like(acc2)
+
     def prepare(q, carry):
         p = pts_v[q].astype(jnp.float32)
         sq = jnp.sum(p * p, axis=1, keepdims=True) * (0.5 / depth)
-        spn[q] = jnp.broadcast_to(sq, (rows, 128))
+        sq = jnp.broadcast_to(sq, (rows, 128))
         lw = jnp.broadcast_to(plogw[pl.ds(q, 1), :], (rows, 128)) * LOG2E
-        l2[q] = jnp.transpose(lw)
+        lw = jnp.transpose(lw)
+        for it in range(iters):
+            base[it, q] = lw + weights[it] * sq
+        acc[...] = jnp.where(lanes == q, sq, acc[...])
         for k in range(keep):
             krow[pl.ds(q * keep + k, 1), :] = jnp.full((1, 128), kept_s[k, q], jnp.int32)
         return carry
 
     lax.fori_loop(0, blocks, prepare, 0)
+    spd[...] = jnp.transpose(acc[...])[:blocks]
 
     def norms(slot):
         for w in range(slot * panel, (slot + 1) * panel):
@@ -180,60 +196,51 @@
     for device in sides:
         pl.semaphore_signal(far, inc=1, device_id=device, device_id_type=MESH)
 
-    strength = relax_s[0]
-    lanes = lax.broadcasted_iota(jnp.int32, (rows, 128), 1)
-    acc[...] = jnp.zeros_like(acc)
-
     def bias(inv_eps, j, pot):
         block = pl.ds(j * panel, panel)
         b2[block, :] = LOG2E * (wlogw[j] + (pot - san[block, :]) * inv_eps)
 
-    def point_lse(q, ratio, brow, strip):
-        t = x_s[q, strip, :]
-        if ratio is not None:
-            t = t * ratio
-            x_s[q, strip, :] = t
-        t = t + brow
-        top = jnp.max(t, axis=1, keepdims=True)
-        total = jnp.sum(jnp.exp2(t - top), axis=1, keepdims=True)
-        return jnp.broadcast_to(top + jnp.log2(total), (STRIP, 128))
-
     def bias_row(q):
         return jnp.concatenate(
             [b2[pl.ds(kept_s[k, q], 1), :] for k in range(keep)], axis=1
         )
 
+    def point_lse(q, brow, strip):
+        t = x_s[q, strip, :] + brow
+        top = jnp.max(t, axis=1, keepdims=True)
+        total = jnp.sum(jnp.exp2(t - top), axis=1, keepdims=True)
+        shape = (STRIP, 128)
+        return jnp.broadcast_to(top, shape), jnp.broadcast_to(total, shape)
+
+    strips = [pl.ds(r * STRIP, STRIP) for r in range(rows // STRIP)]
+
     for it in range(iters):
         eps = eps_s[it]
         inv_eps = jnp.ones((1, 128), jnp.float32) / jnp.full((1, 128), eps, jnp.float32)
-        factor = strength / (strength + eps)
+        factor = factors[it]
         scale = (LOG2E / depth) * inv_eps[0:1, 0:1]
         if it == 0:
             for j in range(3):
                 bias(inv_eps, j, jnp.zeros((panel, 128), jnp.float32))
-        ratio = None if it == 0 else eps_s[it - 1] * inv_eps[0:1, 0:1]
         last = it == iters - 1
 
+        def products(q):
+            ids = [kept_s[k, jnp.minimum(q, blocks - 1)] for k in range(keep)]
+            chosen = jnp.concatenate([win[w] for w in ids], axis=0)
+            x_s[q] = scale * lax.dot_general(
+                pts_v[q],
+                chosen,
+                (((1,), (1,)), ((), ())),
+                preferred_element_type=jnp.float32,
+            )
+
         def one(q):
-            if it == 0:
-                chosen = jnp.concatenate(
-                    [win[kept_s[k, q]] for k in range(keep)], axis=0
+            brow = bias_row(q)
+            for strip in strips:
+                top, total = point_lse(q, brow, strip)
+                a2[q, strip, :] = base[it, q, strip, :] - factor * (
+                    top + jnp.log2(total)
                 )
-                x_s[q] = scale * lax.dot_general(
-                    pts_v[q],
-                    chosen,
-                    (((1,), (1,)), ((), ())),
-                    preferred_element_type=jnp.float32,
-                )
-            brow = bias_row(q)
-            for r in range(rows // STRIP):
-                strip = pl.ds(r * STRIP, STRIP)
-                lse = point_lse(q, ratio, brow, strip)
-                sp = spn[q, strip, :]
-                pot = factor * (sp - (eps * LN2) * lse)
-                a2[q, strip, :] = l2[q, strip, :] + (pot - sp) * (LOG2E * inv_eps)
-                if last:
-                    acc[strip, :] = jnp.where(lanes[:STRIP] == q, pot, acc[strip, :])
             for k in range(keep):
                 u = x_s[q, :, pl.ds(k * 128, 128)] + a2[q]
                 top = jnp.max(u, axis=0, keepdims=True)
@@ -244,8 +251,13 @@
         def step(g, carry):
             for i in range(GROUP):
                 one(g * GROUP + i)
+                if it == 0:
+                    products((g + 1) * GROUP + i)
             return carry
 
+        if it == 0:
+            for i in range(GROUP):
+                products(i)
         lax.fori_loop(0, blocks // GROUP, step, 0)
 
         member, m = krow[...], mrow[...]
@@ -280,7 +292,22 @@
         for copy in copies:
             copy.start()
         if last:
-            pot_out[...] = jnp.transpose(acc[...])[:blocks]
+
+            def gather(q, carry):
+                acc[...] = jnp.where(lanes == q, a2[q], acc[...])
+                return carry
+
+            lax.fori_loop(0, blocks, gather, 0)
+            dense = jnp.transpose(acc[...])[:blocks]
+            pot_out[...] = spd[...] + (dense - LOG2E * plogw[...]) * (eps * LN2)
+        else:
+            ratio = eps / jnp.full((1, 128), eps_s[it + 1], jnp.float32)[0:1, 0:1]
+
+            def rescale(q, carry):
+                x_s[q] = x_s[q] * ratio
+                return carry
+
+            lax.fori_loop(0, blocks, rescale, 0)
         for copy in copies:
             copy.wait()
 
@@ -302,14 +329,16 @@
         for i in range(GROUP):
             q = g * GROUP + i
             brow = bias_row(q)
-            for r in range(rows // STRIP):
-                strip = pl.ds(r * STRIP, STRIP)
-                mass = (point_lse(q, None, brow, strip) + a2[q, strip, :]) * LN2
-                acc[strip, :] = jnp.where(lanes[:STRIP] == q, mass, acc[strip, :])
+            for strip in strips:
+                top, total = point_lse(q, brow, strip)
+                here = lanes[:STRIP] == q
+                acc[strip, :] = jnp.where(here, top, acc[strip, :])
+                acc2[strip, :] = jnp.where(here, total, acc2[strip, :])
         return carry
 
     lax.fori_loop(0, blocks // GROUP, closing, 0)
-    mass_out[...] = jnp.transpose(acc[...])[:blocks]
+    lse = acc[...] + jnp.log2(acc2[...])
+    mass_out[...] = (jnp.transpose(lse)[:blocks] + dense) * LN2
 
 
 def finish(pot, apot, mass, pot_out, apot_out, mass_out, sem):
@@ -353,18 +382,19 @@
             pltpu.SMEM((iters,), f32),
             pltpu.SMEM((1,), f32),
             pltpu.VMEM((blocks, 128), f32),
-            pltpu.VMEM((blocks, 128, depth), bf16),
+            pltpu.VMEM((blocks + GROUP, 128, depth), bf16),
             pltpu.VMEM((3 * panel, 128, depth), bf16),
             pltpu.VMEM((3, panel, 128), f32),
-            pltpu.VMEM((blocks, 128, keep * 128), f32),
+            pltpu.VMEM((blocks + GROUP, 128, keep * 128), f32),
+            pltpu.VMEM((iters, blocks, 128, 128), f32),
             pltpu.VMEM((blocks, 128, 128), f32),
-            pltpu.VMEM((blocks, 128, 128), f32),
-            pltpu.VMEM((blocks, 128, 128), f32),
+            pltpu.VMEM((blocks, 128), f32),
             pltpu.VMEM((blocks * keep, 128), jnp.int32),
             pltpu.VMEM((blocks * keep, 128), f32),
             pltpu.VMEM((blocks * keep, 128), f32),
             pltpu.VMEM((3 * panel, 128), f32),
             pltpu.VMEM((3 * panel, 128), f32),
+            pltpu.VMEM((128, 128), f32),
             pltpu.VMEM((128, 128), f32),
             pltpu.VMEM((iters, 3, panel, 128), f32),
             pltpu.VMEM((iters, 5, npts, 3, panel, 128), f32),

time: 40.5 us -> 38.2 us (0.943)
  Pallas kernels: 39.1 us -> 36.7 us
    pallas_call x1, Pallas kernels: 38.4 us -> 36.1 us  [per_device(): pl.pallas_call(functools.partial(kernel, npts, natom), out_shape=(jax.Sha...]
where the time goes in v2:
time: 38.2 us; the launch traced here: 38 us
  Pallas kernels  36.7 us (96%)
  between operations  1.29 us (3%)
    pallas_call x1, Pallas kernels, per_device(): pl.pallas_call(functools.partial(kernel, npts, natom), out_shape=(jax.Sha...  36.1 us

profile of v2, /device:TPU:0, one launch (start us, length us, event | category | flops | bytes accessed | tf_op | source)
XLA Modules:
  0.0 38.0 jit_solution(5178708873939015263)
XLA Ops:
  1.3 36.1 %shard_map.94 = (f32[32,128]{1,0:T(8,128)S(1)}, f32[4,128]{1,0:T(4,128)S(1)}, f32[32,128]{1,0:T(8,128)S(1)}) custom-call(s32[4,32]{1,0:T(4,128)} %bitcast.11, f32[2]{0:T(128)} %eps_h.1, f32[1]{0:T(128)S(6)} %copy.10.relax_h, bf16[32,128,256]{2,1,0:T(8,128)(2,1)} %bitcast.8, bf16[4,128,256]{2,1,0:T(8,128)(2,1)} %bitcast.9, f32[32,128]{1,0:T(8,128)} %bitcast.10, ...), custom_call_target="tpu_custom_call" | custom-call | tf_op jit(solution)/shard_map/pallas_call | solution.py:371
  37.4 0.6 %shard_map.95 = (f32[32,128]{1,0:T(8,128)}, f32[4,128]{1,0:T(4,128)}, f32[32,128]{1,0:T(8,128)}) custom-call(f32[32,128]{1,0:T(8,128)S(1)} %get-tuple-element.9.pot, f32[4,128]{1,0:T(4,128)S(1)} %get-tuple-element.10.apot, f32[32,128]{1,0:T(8,128)S(1)} %get-tuple-element.11.mass), custom_call_target="tpu_custom_call" | custom-call | tf_op jit(solution)/shard_map/pallas_call | solution.py:425

commit v3 on v2

--- a/solution.py
+++ b/solution.py
@@ -35,7 +35,7 @@
     plogw,
     pts_v,
     win,
-    wlogw,
+    masses,
     x_s,
     base,
     a2,
@@ -44,7 +44,6 @@
     mrow,
     srow,
     b2,
-    san,
     acc,
     acc2,
     part,
@@ -69,6 +68,9 @@
     mine, here = lax.axis_index("pts"), lax.axis_index("atom")
     up, down = lax.rem(here + 1, natom), lax.rem(here + natom - 1, natom)
     core = lax.rem(mine, 2)
+    odd = lax.rem(here, 2)
+    farther = lax.rem(here - 1 + 2 * odd + natom, natom)
+    closer = here + 1 - 2 * odd
     partner = mine + 1 - 2 * core
 
     local = []
@@ -78,7 +80,7 @@
             (plogw_h, plogw),
             (eps_h, eps_s),
             (relax_h, relax_s),
-            (alogw_h, wlogw.at[1]),
+            (alogw_h, masses.at[1, 0]),
             (points_h, pts_v.at[pl.ds(0, blocks)]),
             (atoms_h, win.at[pl.ds(panel, panel)]),
         )
@@ -108,7 +110,7 @@
 
     halo, small = [], []
     mine_half = pl.ds(core * half, half)
-    for side, (slot, to) in enumerate(((0, up), (2, down))):
+    for side, (slot, to) in enumerate(((2 - 2 * odd, farther), (2 * odd, closer))):
         halo.append(
             pltpu.make_async_remote_copy(
                 src_ref=atoms_h.at[mine_half],
@@ -121,19 +123,28 @@
         )
         small.append(
             pltpu.make_async_remote_copy(
-                src_ref=alogw_h,
-                dst_ref=wlogw.at[slot],
+                src_ref=masses.at[1],
+                dst_ref=masses.at[slot],
                 send_sem=gsend.at[side],
                 recv_sem=grecv.at[side],
                 device_id=(mine, to),
                 device_id_type=MESH,
             )
         )
-    for copy in halo + small:
+    for copy in halo:
         copy.start()
 
     for copy in local:
         copy.wait()
+
+    for w in range(panel):
+        a = win[panel + w].astype(jnp.float32)
+        sq = jnp.sum(a * a, axis=1, keepdims=True) * (0.5 / depth)
+        masses[1, 1, pl.ds(w, 1), :] = jnp.transpose(
+            jnp.broadcast_to(sq, (rows, 128))
+        )[0:1, :]
+    for copy in small:
+        copy.start()
 
     lanes = lax.broadcasted_iota(jnp.int32, (rows, 128), 1)
     strength = relax_s[0]
@@ -146,31 +157,28 @@
     acc[...] = jnp.zeros_like(acc)
     acc2[...] = jnp.zeros_like(acc2)
 
-    def prepare(q, carry):
-        p = pts_v[q].astype(jnp.float32)
-        sq = jnp.sum(p * p, axis=1, keepdims=True) * (0.5 / depth)
-        sq = jnp.broadcast_to(sq, (rows, 128))
-        lw = jnp.broadcast_to(plogw[pl.ds(q, 1), :], (rows, 128)) * LOG2E
-        lw = jnp.transpose(lw)
-        for it in range(iters):
-            base[it, q] = lw + weights[it] * sq
-        acc[...] = jnp.where(lanes == q, sq, acc[...])
-        for k in range(keep):
-            krow[pl.ds(q * keep + k, 1), :] = jnp.full((1, 128), kept_s[k, q], jnp.int32)
+    def prepare(g, carry):
+        for i in range(GROUP):
+            q = g * GROUP + i
+            p = pts_v[q].astype(jnp.float32)
+            sq = jnp.sum(p * p, axis=1, keepdims=True) * (0.5 / depth)
+            sq = jnp.broadcast_to(sq, (rows, 128))
+            lw = jnp.broadcast_to(plogw[pl.ds(q, 1), :], (rows, 128)) * LOG2E
+            lw = jnp.transpose(lw)
+            for it in range(iters):
+                base[it, q] = lw + weights[it] * sq
+            acc[...] = jnp.where(lanes == q, sq, acc[...])
+            for k in range(keep):
+                krow[pl.ds(q * keep + k, 1), :] = jnp.full(
+                    (1, 128), kept_s[k, q], jnp.int32
+                )
         return carry
 
-    lax.fori_loop(0, blocks, prepare, 0)
+    lax.fori_loop(0, blocks // GROUP, prepare, 0)
     spd[...] = jnp.transpose(acc[...])[:blocks]
 
-    def norms(slot):
-        for w in range(slot * panel, (slot + 1) * panel):
-            a = win[w].astype(jnp.float32)
-            sq = jnp.sum(a * a, axis=1, keepdims=True) * (0.5 / depth)
-            san[pl.ds(w, 1), :] = jnp.transpose(jnp.broadcast_to(sq, (rows, 128)))[0:1, :]
-
-    norms(1)
     forward = []
-    for side, slot in enumerate((0, 2)):
+    for side, slot in enumerate((2 * odd, 2 - 2 * odd)):
         halo[side].wait_recv()
         piece = pl.ds(slot * panel + core * half, half)
         forward.append(
@@ -184,9 +192,8 @@
             )
         )
         forward[side].start()
-    for side, slot in enumerate((0, 2)):
+    for side in range(2):
         forward[side].wait()
-        norms(slot)
     for copy in halo:
         copy.wait_send()
     for copy in small:
@@ -198,7 +205,7 @@
 
     def bias(inv_eps, j, pot):
         block = pl.ds(j * panel, panel)
-        b2[block, :] = LOG2E * (wlogw[j] + (pot - san[block, :]) * inv_eps)
+        b2[block, :] = LOG2E * (masses[j, 0] + (pot - masses[j, 1]) * inv_eps)
 
     def bias_row(q):
         return jnp.concatenate(
@@ -320,7 +327,7 @@
             top = functools.reduce(jnp.maximum, terms)
             total = functools.reduce(jnp.add, [jnp.exp2(term - top) for term in terms])
             lse = jnp.where(top > 0.5 * lowest, top + jnp.log2(total), -jnp.inf)
-            pot = factor * (san[pl.ds(j * panel, panel), :] - (eps * LN2) * lse)
+            pot = factor * (masses[j, 1] - (eps * LN2) * lse)
             bias(next_inv, j, pot)
             if last and j == 1:
                 apot_out[...] = pot
@@ -384,7 +391,7 @@
             pltpu.VMEM((blocks, 128), f32),
             pltpu.VMEM((blocks + GROUP, 128, depth), bf16),
             pltpu.VMEM((3 * panel, 128, depth), bf16),
-            pltpu.VMEM((3, panel, 128), f32),
+            pltpu.VMEM((3, 2, panel, 128), f32),
             pltpu.VMEM((blocks + GROUP, 128, keep * 128), f32),
             pltpu.VMEM((iters, blocks, 128, 128), f32),
             pltpu.VMEM((blocks, 128, 128), f32),
@@ -392,7 +399,6 @@
             pltpu.VMEM((blocks * keep, 128), jnp.int32),
             pltpu.VMEM((blocks * keep, 128), f32),
             pltpu.VMEM((blocks * keep, 128), f32),
-            pltpu.VMEM((3 * panel, 128), f32),
             pltpu.VMEM((3 * panel, 128), f32),
             pltpu.VMEM((128, 128), f32),
             pltpu.VMEM((128, 128), f32),

time: 38.2 us -> 38 us (level)
  no operation moved by 1% of the time
where the time goes in v3:
time: 38 us; the launch traced here: 37.8 us
  Pallas kernels  36.5 us (96%)
  between operations  1.29 us (3%)
    pallas_call x1, Pallas kernels, per_device(): pl.pallas_call(functools.partial(kernel, npts, natom), out_shape=(jax.Sha...  35.9 us

profile of v3, /device:TPU:0, one launch (start us, length us, event | category | flops | bytes accessed | tf_op | source)
XLA Modules:
  0.0 37.8 jit_solution(12441602785425437444)
XLA Ops:
  1.3 35.9 %shard_map.94 = (f32[32,128]{1,0:T(8,128)S(1)}, f32[4,128]{1,0:T(4,128)S(1)}, f32[32,128]{1,0:T(8,128)S(1)}) custom-call(s32[4,32]{1,0:T(4,128)} %bitcast.11, f32[2]{0:T(128)} %eps_h.1, f32[1]{0:T(128)S(6)} %copy.10.relax_h, bf16[32,128,256]{2,1,0:T(8,128)(2,1)} %bitcast.8, bf16[4,128,256]{2,1,0:T(8,128)(2,1)} %bitcast.9, f32[32,128]{1,0:T(8,128)} %bitcast.10, ...), custom_call_target="tpu_custom_call" | custom-call | tf_op jit(solution)/shard_map/pallas_call | solution.py:378
  37.2 0.6 %shard_map.95 = (f32[32,128]{1,0:T(8,128)}, f32[4,128]{1,0:T(4,128)}, f32[32,128]{1,0:T(8,128)}) custom-call(f32[32,128]{1,0:T(8,128)S(1)} %get-tuple-element.9.pot, f32[4,128]{1,0:T(4,128)S(1)} %get-tuple-element.10.apot, f32[32,128]{1,0:T(8,128)S(1)} %get-tuple-element.11.mass), custom_call_target="tpu_custom_call" | custom-call | tf_op jit(solution)/shard_map/pallas_call | solution.py:431

commit v4 on v3

--- a/solution.py
+++ b/solution.py
@@ -55,6 +55,7 @@
     frecv,
     gsend,
     grecv,
+    volume,
     esend,
     erecv,
     near,
@@ -282,14 +283,14 @@
         rb[it, 2, mine] = part[it]
 
         copies = []
-        for n, (o, t) in enumerate(partners):
+        for o, t in partners:
             low, high = max(0, -o), min(3, 3 - o)
             copies.append(
                 pltpu.make_async_remote_copy(
                     src_ref=part.at[it, pl.ds(low, high - low)],
                     dst_ref=rb.at[it, o + 2, mine, pl.ds(low + o, high - low)],
-                    send_sem=esend.at[it, n],
-                    recv_sem=erecv.at[it, n],
+                    send_sem=esend.at[it],
+                    recv_sem=erecv.at[it],
                     device_id=target(o, t),
                     device_id_type=MESH,
                 )
@@ -315,8 +316,8 @@
                 return carry
 
             lax.fori_loop(0, blocks, rescale, 0)
-        for copy in copies:
-            copy.wait()
+        for sem in (esend, erecv):
+            pltpu.make_async_copy(volume, volume, sem.at[it]).wait()
 
         next_eps = eps_s[min(it + 1, iters - 1)]
         next_inv = jnp.ones((1, 128), jnp.float32) / jnp.full((1, 128), next_eps, jnp.float32)
@@ -368,7 +369,6 @@
     keep = kept.shape[1]
     iters = epsilons.shape[0]
     npts, natom = lax.axis_size("pts"), lax.axis_size("atom")
-    partners = 5 * npts - 1
     f32, bf16 = jnp.float32, jnp.bfloat16
     vmem = pl.BlockSpec(memory_space=pltpu.VMEM)
     hbm = pl.BlockSpec(memory_space=pltpu.HBM)
@@ -411,8 +411,9 @@
             pltpu.SemaphoreType.DMA((2,)),
             pltpu.SemaphoreType.DMA((2,)),
             pltpu.SemaphoreType.DMA((2,)),
-            pltpu.SemaphoreType.DMA((iters, partners)),
-            pltpu.SemaphoreType.DMA((iters, partners)),
+            pltpu.VMEM((9 * npts - 3, panel, 128), f32),
+            pltpu.SemaphoreType.DMA((iters,)),
+            pltpu.SemaphoreType.DMA((iters,)),
             pltpu.SemaphoreType.REGULAR,
             pltpu.SemaphoreType.REGULAR,
         ],

time: 38 us -> 37.3 us (0.982)
  Pallas kernels: 36.5 us -> 35.8 us
    pallas_call x1, Pallas kernels: 35.9 us -> 35.2 us  [per_device(): pl.pallas_call(functools.partial(kernel, npts, natom), out_shape=(jax.Sha...]
where the time goes in v4:
time: 37.3 us; the launch traced here: 37.1 us
  Pallas kernels  35.8 us (96%)
  between operations  1.29 us (3%)
    pallas_call x1, Pallas kernels, per_device(): pl.pallas_call(functools.partial(kernel, npts, natom), out_shape=(jax.Sha...  35.2 us

profile of v4, /device:TPU:0, one launch (start us, length us, event | category | flops | bytes accessed | tf_op | source)
XLA Modules:
  0.0 37.1 jit_solution(8051201083587153342)
XLA Ops:
  1.3 35.2 %shard_map.94 = (f32[32,128]{1,0:T(8,128)S(1)}, f32[4,128]{1,0:T(4,128)S(1)}, f32[32,128]{1,0:T(8,128)S(1)}) custom-call(s32[4,32]{1,0:T(4,128)} %bitcast.11, f32[2]{0:T(128)} %eps_h.1, f32[1]{0:T(128)S(6)} %copy.10.relax_h, bf16[32,128,256]{2,1,0:T(8,128)(2,1)} %bitcast.8, bf16[4,128,256]{2,1,0:T(8,128)(2,1)} %bitcast.9, f32[32,128]{1,0:T(8,128)} %bitcast.10, ...), custom_call_target="tpu_custom_call" | custom-call | tf_op jit(solution)/shard_map/pallas_call | solution.py:378
  36.4 0.6 %shard_map.95 = (f32[32,128]{1,0:T(8,128)}, f32[4,128]{1,0:T(4,128)}, f32[32,128]{1,0:T(8,128)}) custom-call(f32[32,128]{1,0:T(8,128)S(1)} %get-tuple-element.9.pot, f32[4,128]{1,0:T(4,128)S(1)} %get-tuple-element.10.apot, f32[32,128]{1,0:T(8,128)S(1)} %get-tuple-element.11.mass), custom_call_target="tpu_custom_call" | custom-call | tf_op jit(solution)/shard_map/pallas_call | solution.py:432

commit v5 on v4

--- a/solution.py
+++ b/solution.py
@@ -91,7 +91,7 @@
         copy.start()
 
     partners = []
-    for o in (-2, -1, 0, 1, 2):
+    for o in (-2, 2, -1, 1, 0):
         for t in range(npts):
             if o == 0 and t == 0:
                 continue

time: 37.3 us -> 37.4 us (level)
  no operation moved by 1% of the time
where the time goes in v5:
time: 37.4 us; the launch traced here: 37.2 us
  Pallas kernels  36 us (96%)
  between operations  1.29 us (3%)
    pallas_call x1, Pallas kernels, per_device(): pl.pallas_call(functools.partial(kernel, npts, natom), out_shape=(jax.Sha...  35.3 us

profile of v5, /device:TPU:0, one launch (start us, length us, event | category | flops | bytes accessed | tf_op | source)
XLA Modules:
  0.0 37.2 jit_solution(4008020162728507116)
XLA Ops:
  1.3 35.3 %shard_map.94 = (f32[32,128]{1,0:T(8,128)S(1)}, f32[4,128]{1,0:T(4,128)S(1)}, f32[32,128]{1,0:T(8,128)S(1)}) custom-call(s32[4,32]{1,0:T(4,128)} %bitcast.11, f32[2]{0:T(128)} %eps_h.1, f32[1]{0:T(128)S(6)} %copy.10.relax_h, bf16[32,128,256]{2,1,0:T(8,128)(2,1)} %bitcast.8, bf16[4,128,256]{2,1,0:T(8,128)(2,1)} %bitcast.9, f32[32,128]{1,0:T(8,128)} %bitcast.10, ...), custom_call_target="tpu_custom_call" | custom-call | tf_op jit(solution)/shard_map/pallas_call | solution.py:378
  36.6 0.6 %shard_map.95 = (f32[32,128]{1,0:T(8,128)}, f32[4,128]{1,0:T(4,128)}, f32[32,128]{1,0:T(8,128)}) custom-call(f32[32,128]{1,0:T(8,128)S(1)} %get-tuple-element.9.pot, f32[4,128]{1,0:T(4,128)S(1)} %get-tuple-element.10.apot, f32[32,128]{1,0:T(8,128)S(1)} %get-tuple-element.11.mass), custom_call_target="tpu_custom_call" | custom-call | tf_op jit(solution)/shard_map/pallas_call | solution.py:432
